TPU v7x, 32 devices: a whole 2x2x4 slice. The times are simulated.
32 devices in a mesh: groups: 2 (over x), seq: 8 (over z, y), head: 2 (over core).
Axes of the slice: x: 2, y: 2, z: 4, core: 2. Of those that a mesh axis runs over, the one named last changes fastest.
Arguments:
- queries: bfloat16 [8192, 2048], P(('groups', 'seq'), 'head'), parts along dimension 0, may hold values from -6 to 6
- keys: bfloat16 [8192, 1024], P(('groups', 'seq'), 'head'), parts along dimension 0, may hold values from -6 to 6
- values: bfloat16 [8192, 1024], P(('groups', 'seq'), 'head'), parts along dimension 0, may hold values from -6 to 6
- segments: int32 [8192], P('groups'), parts along dimension 0, may hold values from 0 to 7, never falling along the last dimension, each value on 1 to 1024 neighbouring positions
- out_weight: bfloat16 [2048, 5376], P('head'), may hold values from -0.125 to 0.125
Outputs:
- mixed: bfloat16 [8192, 5376], P(('groups', 'seq')), parts along dimension 0
There are 2 independent parts, one for each index of `groups`. A program takes and returns all parts, laid end to end along the dimension named above; an argument that names none is the same for every part. Nothing has to cross between parts.
Inputs may be any that keep to these rules, and one draw needn't show every extreme that they name: `segments`: document ids never fall along the slab; each document has 1 to 1024 tokens, one exactly 1024.
All inputs are finite; a program needn't handle non-finite values.
Results may differ from a plain program's by a relative error of at most 0.011.
Values may be sent and summed in bfloat16 or wider, within the bound.
A program may use at most 128 MiB of HBM per device.

v0:
```python
import math

import jax
import jax.numpy as jnp
from jax import lax
from jax.sharding import PartitionSpec as P

HEAD_SIZE = 128
SCALAR = 168
ATTENTION_SPAN = 1024
HALO = 2


def from_behind(value, axis, by):
    peers = lax.axis_size(axis)
    pairs = [(i, i + by) for i in range(peers) if 0 <= i + by < peers]
    return lax.ppermute(value, axis, pairs)


def shards(queries, keys, values, segments, out_weight):
    tok_rows = queries.shape[0]
    heads_kv = keys.shape[1] // HEAD_SIZE
    query_group = queries.shape[1] // keys.shape[1]
    seq_index = lax.axis_index("seq")
    pieces = []
    for distance in range(HALO, 0, -1):
        pieces.append(from_behind((keys, values), "seq", distance))
    keys_ext = jnp.concatenate([piece[0] for piece in pieces] + [keys], axis=0)
    values_ext = jnp.concatenate([piece[1] for piece in pieces] + [values], axis=0)
    window_span = keys_ext.shape[0]
    first_row = seq_index * tok_rows
    pad_segments = jnp.concatenate([jnp.full((HALO * tok_rows,), -1, jnp.int32), segments])
    seg_key = lax.dynamic_slice_in_dim(pad_segments, first_row, window_span, 0)
    seg_query = lax.dynamic_slice_in_dim(segments, first_row, tok_rows, 0)
    key_pos = first_row - HALO * tok_rows + jnp.arange(window_span, dtype=jnp.int32)
    key_mat = keys_ext.reshape(window_span, heads_kv, HEAD_SIZE)
    value_mat = values_ext.reshape(window_span, heads_kv, HEAD_SIZE)
    token_block = math.gcd(tok_rows, 512)

    def one_block(block_id):
        start = block_id * token_block
        query_block = queries.reshape(token_block, heads_kv, query_group, HEAD_SIZE)
        query_pos = first_row + start + jnp.arange(token_block, dtype=jnp.int32)
        allowed = (
            (key_pos[None, :] <= query_pos[:, None])
            & (query_pos[:, None] - key_pos[None, :] < ATTENTION_SPAN)
            & (seg_key[None, :] == seg_query[:, None])
        )
        scores = jnp.einsum(
            "qkgd,pkd->kgqp", query_block, key_mat, preferred_element_type=jnp.float32
        ) * SCALAR ** (-0.5)
        masked = jnp.where(allowed, scores, -1e30)
        row_max = jnp.max(masked, axis=-1, keepdims=True)
        expo = jnp.where(allowed, jnp.exp(masked - row_max), 0.0)
        weights = (expo / jnp.sum(expo, axis=-1, keepdims=True)).astype(jnp.bfloat16)
        heads_out = jnp.einsum(
            "kgqp,pkd->qkgd", weights, value_mat, preferred_element_type=jnp.float32
        )
        return heads_out.astype(jnp.bfloat16).reshape(
            token_block, heads_kv * query_group * HEAD_SIZE
        )

    attended = lax.map(one_block, jnp.arange(tok_rows // token_block, dtype=jnp.int32)).reshape(
        tok_rows, -1
    )
    partial_terms = jnp.dot(attended, out_weight, preferred_element_type=jnp.float32)
    mixed = lax.psum(partial_terms, "head").astype(jnp.bfloat16)
    return mixed


def solution(mesh):
    placed = (
        P(("groups", "seq"), "head"),
        P(("groups", "seq"), "head"),
        P(("groups", "seq"), "head"),
        P("groups"),
        P("head", None),
    )
    return jax.shard_map(
        shards, mesh=mesh, in_specs=placed, out_specs=P(("groups", "seq"), None), check_vma=False
    )
```

profile of v0, /device:TPU:17, one launch (start us, length us, event | category | flops | bytes accessed | tf_op | source)
XLA Modules:
  0.0 131.4 jit_solution(17479699707473325721)
XLA Ops:
  0.0 1.3 copy.10
  1.3 3.1 %collective-permute-start.3 = (bf16[512,512]{0,1:T(8,128)(2,1)S(1)}, bf16[512,512]{0,1:T(8,128)(2,1)}, u32[]{:S(2)}, u32[]{:S(2)}) collective-permute-start(bf16[512,512]{0,1:T(8,128)(2,1)S(1)} %copy.10), channel_id=1, source_target_pairs={{0,2},{2,4},{4,6},{6,8},{8,10},{10,12},{12,14},{1,3},{3,5},{5,7},{... | collective-permute-start | bytes 1572872 | tf_op jit(solution)/shard_map/ppermute | solution.py:17
  4.4 3.2 %collective-permute-start.2 = (bf16[512,512]{0,1:T(8,128)(2,1)S(1)}, bf16[512,512]{0,1:T(8,128)(2,1)}, u32[]{:S(2)}, u32[]{:S(2)}) collective-permute-start(bf16[512,512]{0,1:T(8,128)(2,1)S(1)} %copy.10), channel_id=1, source_target_pairs={{0,4},{2,6},{4,8},{6,10},{8,12},{10,14},{1,5},{3,7},{5,9},{7,11},{... | collective-permute-start | bytes 1572872 | tf_op jit(solution)/shard_map/ppermute | solution.py:17
  7.6 1.9 %collective-permute-start = (bf16[512,512]{1,0:T(8,128)(2,1)}, bf16[512,512]{1,0:T(8,128)(2,1)S(1)}, u32[]{:S(2)}, u32[]{:S(2)}) collective-permute-start(bf16[512,512]{1,0:T(8,128)(2,1)} %param.7), channel_id=1, source_target_pairs={{0,4},{2,6},{4,8},{6,10},{8,12},{10,14},{1,5},{3,7},{5,9},{7,11},{... | collective-permute-start | bytes 1572872 | tf_op jit(solution)/shard_map/ppermute | solution.py:17
  9.6 1.9 %collective-permute-start.1 = (bf16[512,512]{1,0:T(8,128)(2,1)}, bf16[512,512]{1,0:T(8,128)(2,1)}, u32[]{:S(2)}, u32[]{:S(2)}) collective-permute-start(bf16[512,512]{1,0:T(8,128)(2,1)} %param.7), channel_id=1, source_target_pairs={{0,2},{2,4},{4,6},{6,8},{8,10},{10,12},{12,14},{1,3},{3,5},{5,7},{... | collective-permute-start | bytes 1572872 | tf_op jit(solution)/shard_map/ppermute | solution.py:17
  11.5 0.8 pad_dynamic-slice_fusion
  12.3 0.8 dynamic_slice.10
  13.1 1.9 %fusion.9 = pred[512,1536]{0,1:T(8,128)(4,1)} fusion(s32[512]{0:T(512)S(1)} %dynamic_slice.10, s32[512]{0:T(512)S(1)} %iota_add_fusion.1, s32[1536]{0:T(1024)S(1)} %get-tuple-element.21, s32[1536]{0:T(1024)S(1)} %get-tuple-element.22), kind=kLoop, calls=%fused_computation.12 | loop fusion | flops 4718592 | bytes 802816 | tf_op jit(solution)/shard_map/while/body/eval_jaxpr/and | solution.py:45
  14.9 1.8 %reshape.31 = bf16[512,4,2,128]{3,2,1,0:T(2,128)(2,1)S(1)} reshape(bf16[512,1024]{1,0:T(8,128)(2,1)} %param.5) | data formatting | bytes 2097152 | tf_op jit(solution)/shard_map/while/body/eval_jaxpr/reshape | solution.py:42
  16.7 0.0 copy-start.1
  16.7 13.3 %collective-permute-done = bf16[512,512]{1,0:T(8,128)(2,1)S(1)} collective-permute-done((bf16[512,512]{1,0:T(8,128)(2,1)}, bf16[512,512]{1,0:T(8,128)(2,1)S(1)}, u32[]{:S(2)}, u32[]{:S(2)}) %collective-permute-start) | collective-permute-done | bytes 524320 | tf_op jit(solution)/shard_map/ppermute | solution.py:17
  30.1 0.0 copy-start.2
  30.1 0.8 copy-done.2
  30.9 19.8 %collective-permute-done.1 = bf16[512,512]{1,0:T(8,128)(2,1)} collective-permute-done((bf16[512,512]{1,0:T(8,128)(2,1)}, bf16[512,512]{1,0:T(8,128)(2,1)}, u32[]{:S(2)}, u32[]{:S(2)}) %collective-permute-start.1) | collective-permute-done | bytes 524320 | tf_op jit(solution)/shard_map/ppermute | solution.py:17
  50.7 1.5 %pad_maximum_fusion = bf16[1536,512]{1,0:T(8,128)(2,1)S(1)} fusion(bf16[512,512]{1,0:T(8,128)(2,1)} %param.7, bf16[512,512]{1,0:T(8,128)(2,1)} %collective-permute-done.1, bf16[512,512]{1,0:T(8,128)(2,1)} %copy-done.2), kind=kLoop, calls=%fused_computation.13 | loop fusion | flops 4718592 | bytes 3145728 | tf_op jit(solution)/shard_map/concatenate | solution.py:29
  52.1 1.6 %copy.9 = bf16[1536,512]{0,1:T(8,128)(2,1)} copy(bf16[1536,512]{1,0:T(8,128)(2,1)S(1)} %pad_maximum_fusion) | data formatting | bytes 3145728 | tf_op jit(solution)/shard_map/concatenate | solution.py:29
  53.7 0.0 collective-permute-done.3
  53.7 0.0 collective-permute-done.2
  53.7 2.5 %pad_maximum_fusion.1 = bf16[1536,512]{0,1:T(8,128)(2,1)} fusion(bf16[512,512]{0,1:T(8,128)(2,1)S(1)} %copy.10, bf16[512,512]{0,1:T(8,128)(2,1)} %collective-permute-done.3, bf16[512,512]{0,1:T(8,128)(2,1)} %collective-permute-done.2), kind=kLoop, calls=%fused_computation.14 | loop fusion | flops 4718592 | bytes 3145728 | tf_op jit(solution)/shard_map/concatenate | solution.py:28
  56.2 0.0 copy-done.1
  56.2 0.0 copy-start
  56.2 13.4 %fusion.28 = f32[4,2,512]{2,1,0:T(2,128)S(1)} fusion(pred[512,1536]{0,1:T(8,128)(4,1)} %fusion.9, bf16[1536,4,128,1]{0,2,3,1:T(8,128)(2,1)} %bitcast.32, bf16[512,4,2,128]{3,2,1,0:T(2,128)(2,1)S(1)} %reshape.31), kind=kOutput, calls=%fused_computation.29 | convolution fusion | flops 1642071552 | bytes 3424256 | tf_op jit(solution)/shard_map/while/body/eval_jaxpr/sub | solution.py:54
  69.6 0.0 copy-done
  69.6 15.7 %fusion.10 = bf16[4,128,2,512]{3,1,2,0:T(8,128)(2,1)S(1)} fusion(bf16[1536,4,128,1]{0,2,3,1:T(8,128)(2,1)S(1)} %bitcast.31, f32[4,2,512]{2,1,0:T(2,128)S(1)} %fusion.28, pred[512,1536]{0,1:T(8,128)(4,1)} %fusion.9, bf16[1536,4,128,1]{0,2,3,1:T(8,128)(2,1)} %bitcast.33, bf16[512,4,2,128]{3,2,1,0:T(2,128)(2,1)} %copy-done.1), kind=kOutput, calls=%fused_computation.15 | convolution fusion | flops 3259504128 | bytes 6045696 | tf_op jit(solution)/shard_map/while/body/eval_jaxpr/kgqp,pkd->qkgd/dot_general | solution.py:56
  85.4 12.7 %fusion.31 = f32[512,5376]{1,0:T(8,128)} fusion(bf16[512,1024]{0,1:T(8,128)(2,1)S(1)} %bitcast.34, bf16[1024,5376]{1,0:T(8,128)(2,1)} %param.9), kind=kOutput, calls=%fused_computation.30 | convolution fusion | flops 5637144576 | bytes 23068672 | tf_op jit(solution)/shard_map/dot_general | solution.py:66
  98.1 33.3 %all-reduce.2 = bf16[512,5376]{1,0:T(8,128)(2,1)} all-reduce(f32[512,5376]{1,0:T(8,128)} %fusion.31), channel_id=1, replica_groups=mesh['groups'=2,'seq'=8,'head'=2] {'head'}, use_global_device_ids=true, to_apply=%region_2.3 | all-reduce | flops 2752512 | bytes 16515072 | tf_op jit(solution)/shard_map/psum | solution.py:67
  (1 shorter events, 0.0 us)
Async XLA Ops:
  1.3 52.5 %collective-permute-start.3 = (bf16[512,512]{0,1:T(8,128)(2,1)S(1)}, bf16[512,512]{0,1:T(8,128)(2,1)}, u32[]{:S(2)}, u32[]{:S(2)}) collective-permute-start(bf16[512,512]{0,1:T(8,128)(2,1)S(1)} %copy.10), channel_id=1, source_target_pairs={{0,2},{2,4},{4,6},{6,8},{8,10},{10,12},{12,14},{1,3},{3,5},{5,7},{... | collective-permute-start | bytes 1572872 | tf_op jit(solution)/shard_map/ppermute | solution.py:17
  4.4 49.3 %collective-permute-start.2 = (bf16[512,512]{0,1:T(8,128)(2,1)S(1)}, bf16[512,512]{0,1:T(8,128)(2,1)}, u32[]{:S(2)}, u32[]{:S(2)}) collective-permute-start(bf16[512,512]{0,1:T(8,128)(2,1)S(1)} %copy.10), channel_id=1, source_target_pairs={{0,4},{2,6},{4,8},{6,10},{8,12},{10,14},{1,5},{3,7},{5,9},{7,11},{... | collective-permute-start | bytes 1572872 | tf_op jit(solution)/shard_map/ppermute | solution.py:17
  7.6 22.4 %collective-permute-start = (bf16[512,512]{1,0:T(8,128)(2,1)}, bf16[512,512]{1,0:T(8,128)(2,1)S(1)}, u32[]{:S(2)}, u32[]{:S(2)}) collective-permute-start(bf16[512,512]{1,0:T(8,128)(2,1)} %param.7), channel_id=1, source_target_pairs={{0,4},{2,6},{4,8},{6,10},{8,12},{10,14},{1,5},{3,7},{5,9},{7,11},{... | collective-permute-start | bytes 1572872 | tf_op jit(solution)/shard_map/ppermute | solution.py:17
  9.6 41.1 %collective-permute-start.1 = (bf16[512,512]{1,0:T(8,128)(2,1)}, bf16[512,512]{1,0:T(8,128)(2,1)}, u32[]{:S(2)}, u32[]{:S(2)}) collective-permute-start(bf16[512,512]{1,0:T(8,128)(2,1)} %param.7), channel_id=1, source_target_pairs={{0,2},{2,4},{4,6},{6,8},{8,10},{10,12},{12,14},{1,3},{3,5},{5,7},{... | collective-permute-start | bytes 1572872 | tf_op jit(solution)/shard_map/ppermute | solution.py:17
  16.7 39.4 %copy-start.1 = (bf16[512,4,2,128]{3,2,1,0:T(2,128)(2,1)}, bf16[512,4,2,128]{3,2,1,0:T(2,128)(2,1)S(1)}, u32[]{:S(2)}) copy-start(bf16[512,4,2,128]{3,2,1,0:T(2,128)(2,1)S(1)} %reshape.31) | copy-start | bytes 3145732
  30.1 0.8 copy-start.2
  56.2 13.4 %copy-start = (bf16[1536,512]{0,1:T(8,128)(2,1)S(1)}, bf16[1536,512]{0,1:T(8,128)(2,1)}, u32[]{:S(2)}) copy-start(bf16[1536,512]{0,1:T(8,128)(2,1)} %copy.9) | copy-start | bytes 4718596
where the time goes:
time: 132 us; the launch traced here: 131 us
  matrix products  41.9 us (32%)
  blocking collectives  33.3 us (25%)
  waiting for transfers between devices  33.1 us (25%)
  starting transfers between devices  10.2 us (8%)
  other arithmetic  6.6 us (5%)
  local copies, waits for them, and re-layouts  6.17 us (5%)
    psum x1, blocking collectives, shards(): mixed = lax.psum(partial_terms, 'head').astype(jnp.bfloat16)  33.3 us
    ppermute x4, waiting for transfers between devices, from_behind(): return lax.ppermute(value, axis, pairs)  33.1 us
    dot_general x1, matrix products, one_block(): jnp.einsum('kgqp,pkd->qkgd', weights, value_mat, preferred_element_type=j...  15.7 us
    sub x1, matrix products, one_block(): expo = jnp.where(allowed, jnp.exp(masked - row_max), 0.0)  13.4 us
    dot_general x1, matrix products, shards(): jnp.dot(attended, out_weight, preferred_element_type=jnp.float32)  12.7 us
    ppermute x4, starting transfers between devices, from_behind(): return lax.ppermute(value, axis, pairs)  10.2 us
  transfers between devices with their start and end apart: 4, of which 2 were waited for; matrix products, arithmetic and copies ran while one was open for 6% of the time, Pallas kernels for 0%

commit v1 on v0

v1 whole, which is shorter than its diff:
```python
import functools

import jax
import jax.numpy as jnp
from jax import lax
from jax.experimental import pallas as pl
from jax.experimental.pallas import tpu as pltpu
from jax.sharding import PartitionSpec as P

HEAD_SIZE = 128
SCALAR = 168
ATTENTION_SPAN = 1024
LOG2E = 1.4426950408889634
QUERY_TILE = 256
MESH = pl.DeviceIdType.MESH


def column_chunks(width):
    step = 768
    return [(at, min(step, width - at)) for at in range(0, width, step)]


def kernel(
    q_hbm, k_hbm, v_hbm, seg_ref, w_hbm, out_hbm,
    q_s, k_s, v_s, w_own, w_peer, att_own, att_peer, acc, stage, bias,
    q_sem, kv_sem, w_sem, ws_sem, wr_sem, zs_sem, zr_sem, ys_sem, yr_sem,
    as_sem, ar_sem, ol_sem, os_sem, or_sem,
):
    heads = k_s.shape[0]
    group = q_s.shape[0] // heads
    rows = q_s.shape[1]
    half = w_own.shape[1]
    seq = lax.axis_index("seq")
    core = lax.axis_index("head")
    peers = lax.axis_size("seq")
    odd = lax.rem(seq, 2)
    pair = seq + 1 - 2 * odd
    other = 1 - core
    chunks = column_chunks(half)

    def local_kv(which, h):
        src, dst = ((k_hbm, k_s), (v_hbm, v_s))[which]
        return pltpu.make_async_copy(
            src.at[:, pl.ds(h * HEAD_SIZE, HEAD_SIZE)],
            dst.at[h, pl.ds(2 * rows, rows), :], kv_sem.at[which, h])

    def local_q(n):
        return pltpu.make_async_copy(
            q_hbm.at[:, pl.ds(n * HEAD_SIZE, HEAD_SIZE)], q_s.at[n], q_sem.at[n])

    def far(which, h):
        src, dst = ((k_hbm, k_s), (v_hbm, v_s))[which]
        return pltpu.make_async_remote_copy(
            src_ref=src.at[:, pl.ds(h * HEAD_SIZE, HEAD_SIZE)],
            dst_ref=dst.at[h, pl.ds(0, rows), :],
            send_sem=zs_sem.at[which, h], recv_sem=zr_sem.at[which, h],
            device_id={"seq": seq + 2}, device_id_type=MESH)

    def near(which, h):
        src, dst = ((k_hbm, k_s), (v_hbm, v_s))[which]
        return pltpu.make_async_remote_copy(
            src_ref=src.at[:, pl.ds(h * HEAD_SIZE, HEAD_SIZE)],
            dst_ref=dst.at[h, pl.ds(rows, rows), :],
            send_sem=ys_sem.at[which, h], recv_sem=yr_sem.at[which, h],
            device_id={"seq": pair}, device_id_type=MESH)

    def relay(which, h):
        dst = (k_s, v_s)[which]
        return pltpu.make_async_remote_copy(
            src_ref=dst.at[h, pl.ds(0, rows), :],
            dst_ref=dst.at[h, pl.ds(rows, rows), :],
            send_sem=ys_sem.at[which, h], recv_sem=yr_sem.at[which, h],
            device_id={"seq": pair}, device_id_type=MESH)

    def weight_send():
        return pltpu.make_async_remote_copy(
            src_ref=w_hbm.at[:, pl.ds(pl.multiple_of(other * half, HEAD_SIZE), half)],
            dst_ref=w_peer, send_sem=ws_sem, recv_sem=wr_sem,
            device_id={"head": other}, device_id_type=MESH)

    def weight_local():
        return pltpu.make_async_copy(
            w_hbm.at[:, pl.ds(pl.multiple_of(core * half, HEAD_SIZE), half)], w_own, w_sem)

    def attended_send(h):
        return pltpu.make_async_remote_copy(
            src_ref=att_own.at[h], dst_ref=att_peer.at[h],
            send_sem=as_sem.at[h], recv_sem=ar_sem.at[h],
            device_id={"head": other}, device_id_type=MESH)

    def out_view(at, width, owner):
        return out_hbm.at[:, pl.ds(pl.multiple_of(owner * half + at, HEAD_SIZE), width)]

    def out_local(n):
        at, width = chunks[n]
        return pltpu.make_async_copy(
            stage.at[:, pl.ds(at, width)], out_view(at, width, core), ol_sem.at[n])

    def out_send(n):
        at, width = chunks[n]
        return pltpu.make_async_remote_copy(
            src_ref=stage.at[:, pl.ds(at, width)], dst_ref=out_view(at, width, core),
            send_sem=os_sem.at[n], recv_sem=or_sem.at[n],
            device_id={"head": other}, device_id_type=MESH)

    has_up = seq + 2 < peers
    has_down = seq >= 2
    even = odd == 0
    sends_near = jnp.logical_or(even, seq >= 3)
    relays = jnp.logical_and(jnp.logical_not(even), seq >= 3)
    gets_near = seq >= 1

    barrier = pltpu.get_barrier_semaphore()
    pl.semaphore_signal(barrier, inc=1, device_id={"head": other}, device_id_type=MESH)
    pl.semaphore_signal(barrier, inc=1, device_id={"seq": pair}, device_id_type=MESH)

    @pl.when(has_up)
    def _():
        pl.semaphore_signal(barrier, inc=1, device_id={"seq": seq + 2}, device_id_type=MESH)

    @pl.when(has_down)
    def _():
        pl.semaphore_signal(barrier, inc=1, device_id={"seq": seq - 2}, device_id_type=MESH)

    pl.semaphore_wait(
        barrier, 2 + jnp.minimum(peers - 1 - seq, 2) // 2 + jnp.minimum(seq, 2) // 2)

    for h in range(heads):
        for which in range(2):
            @pl.when(has_up)
            def _():
                far(which, h).start()

            @pl.when(even)
            def _():
                near(which, h).start()

    for h in range(heads):
        for which in range(2):
            local_kv(which, h).start()
        for g in range(group):
            local_q(h * group + g).start()
    weight_send().start()
    weight_local().start()

    @pl.when(jnp.logical_not(has_down))
    def _():
        k_s[:, 0:rows, :] = jnp.zeros((heads, rows, HEAD_SIZE), k_s.dtype)
        v_s[:, 0:rows, :] = jnp.zeros((heads, rows, HEAD_SIZE), v_s.dtype)

    @pl.when(jnp.logical_not(gets_near))
    def _():
        k_s[:, rows:2 * rows, :] = jnp.zeros((heads, rows, HEAD_SIZE), k_s.dtype)
        v_s[:, rows:2 * rows, :] = jnp.zeros((heads, rows, HEAD_SIZE), v_s.dtype)

    tile = QUERY_TILE
    span = ATTENTION_SPAN + tile
    seg_own = seg_ref[seq]
    seg_all = jnp.concatenate(
        [seg_ref[jnp.maximum(seq - 2, 0)], seg_ref[jnp.maximum(seq - 1, 0)], seg_own], axis=1)
    for b in range(rows // tile):
        seg_key = seg_all[:, b * tile:b * tile + span]
        for part in range(tile // 128):
            lo = b * tile + part * 128
            seg_query = jnp.broadcast_to(
                seg_own[:, lo:lo + 128].astype(jnp.float32), (128, 128)).T[:, :1]
            r = part * 128 + lax.broadcasted_iota(jnp.int32, (128, span), 0)
            c = lax.broadcasted_iota(jnp.int32, (128, span), 1)
            position = seq * rows - ATTENTION_SPAN + b * tile + c
            allowed = (
                (c <= r + ATTENTION_SPAN) & (c > r) & (position >= 0)
                & (seg_key.astype(jnp.float32) == seg_query)
            )
            bias[b, part * 128:(part + 1) * 128, :] = jnp.where(allowed, 0.0, -1e30)

    factor = SCALAR ** (-0.5) * LOG2E
    ones = jnp.ones((span, HEAD_SIZE), jnp.bfloat16)

    def product(first, last, at, width):
        own = jnp.concatenate([att_own[n] for n in range(first, last)], axis=1)
        far_side = jnp.concatenate([att_peer[n] for n in range(first, last)], axis=1)
        top = slice(first * group * HEAD_SIZE, last * group * HEAD_SIZE)
        cols = slice(at, at + width)
        return jnp.dot(own, w_own[top, cols], preferred_element_type=jnp.float32) + jnp.dot(
            far_side, w_peer[top, cols], preferred_element_type=jnp.float32)

    def step(h, carry):
        @pl.when(h == heads - 1)
        def _():
            weight_local().wait()
            weight_send().wait_recv()
            for n in range(heads - 1):
                attended_send(n).wait_recv()
            for at, width in chunks:
                acc[:, at:at + width] = product(0, heads - 1, at, width)

        for which in range(2):
            @pl.when(has_down)
            def _():
                far(which, h).wait_recv()

            @pl.when(relays)
            def _():
                relay(which, h).start()

        for which in range(2):
            local_kv(which, h).wait()

            @pl.when(gets_near)
            def _():
                near(which, h).wait_recv()
        for g in range(group):
            local_q(h * group + g).wait()
        for b in range(rows // tile):
            key = k_s[h, b * tile:b * tile + span, :]
            value = jnp.concatenate([v_s[h, b * tile:b * tile + span, :], ones], axis=1)
            for g in range(group):
                query = q_s[h * group + g, b * tile:(b + 1) * tile, :]
                scores = lax.dot_general(
                    query, key, (((1,), (1,)), ((), ())), preferred_element_type=jnp.float32)
                scores = scores + bias[b]
                top = jnp.max(scores, axis=1, keepdims=True)
                weights = jnp.exp2((scores - top) * factor).astype(jnp.bfloat16)
                mix = jnp.dot(weights, value, preferred_element_type=jnp.float32)
                att_own[h, b * tile:(b + 1) * tile, g * HEAD_SIZE:(g + 1) * HEAD_SIZE] = (
                    mix[:, :HEAD_SIZE] / mix[:, HEAD_SIZE:]).astype(jnp.bfloat16)
        attended_send(h).start()
        return carry

    lax.fori_loop(0, heads, step, 0)

    attended_send(heads - 1).wait_recv()
    for n, (at, width) in enumerate(chunks):
        stage[:, at:at + width] = (
            acc[:, at:at + width] + product(heads - 1, heads, at, width)).astype(jnp.bfloat16)
        out_local(n).start()
        out_send(n).start()

    for h in range(heads):
        attended_send(h).wait_send()
        for which in range(2):
            @pl.when(has_up)
            def _():
                far(which, h).wait_send()

            @pl.when(sends_near)
            def _():
                near(which, h).wait_send()
    weight_send().wait_send()
    for n in range(len(chunks)):
        out_local(n).wait()
        out_send(n).wait()


def shards(queries, keys, values, segments, out_weight):
    rows = queries.shape[0]
    assert 2 * rows == ATTENTION_SPAN
    heads = keys.shape[1] // HEAD_SIZE
    query_heads = queries.shape[1] // HEAD_SIZE
    group = query_heads // heads
    width = out_weight.shape[1]
    half = width // 2
    pieces = len(column_chunks(half))
    seg = segments.reshape(segments.shape[0] // rows, 1, rows)
    dma = pltpu.SemaphoreType.DMA
    anywhere = pl.BlockSpec(memory_space=pl.ANY)
    bf16 = jnp.bfloat16
    span = ATTENTION_SPAN + QUERY_TILE
    return pl.pallas_call(
        kernel,
        out_shape=jax.ShapeDtypeStruct((rows, width), bf16),
        in_specs=[anywhere, anywhere, anywhere, pl.BlockSpec(memory_space=pltpu.VMEM), anywhere],
        out_specs=anywhere,
        scratch_shapes=[
            pltpu.VMEM((query_heads, rows, HEAD_SIZE), bf16),
            pltpu.VMEM((heads, 3 * rows, HEAD_SIZE), bf16),
            pltpu.VMEM((heads, 3 * rows, HEAD_SIZE), bf16),
            pltpu.VMEM((out_weight.shape[0], half), bf16),
            pltpu.VMEM((out_weight.shape[0], half), bf16),
            pltpu.VMEM((heads, rows, group * HEAD_SIZE), bf16),
            pltpu.VMEM((heads, rows, group * HEAD_SIZE), bf16),
            pltpu.VMEM((rows, half), jnp.float32),
            pltpu.VMEM((rows, half), bf16),
            pltpu.VMEM((rows // QUERY_TILE, QUERY_TILE, span), jnp.float32),
            dma((query_heads,)), dma((2, heads)), dma, dma, dma,
            dma((2, heads)), dma((2, heads)), dma((2, heads)), dma((2, heads)),
            dma((heads,)), dma((heads,)), dma((pieces,)), dma((pieces,)), dma((pieces,)),
        ],
        compiler_params=pltpu.CompilerParams(
            collective_id=0, has_side_effects=True, vmem_limit_bytes=56 * 1024 * 1024),
    )(queries, keys, values, seg, out_weight)


def solution(mesh):
    placed = (
        P(("groups", "seq"), "head"),
        P(("groups", "seq"), "head"),
        P(("groups", "seq"), "head"),
        P("groups"),
        P("head", None),
    )
    return jax.shard_map(
        shards, mesh=mesh, in_specs=placed, out_specs=P(("groups", "seq"), None), check_vma=False
    )
```

time: 132 us -> 52.4 us (0.40)
  Pallas kernels: 0 us -> 46.8 us
  matrix products: 41.9 us -> 0 us
  blocking collectives: 33.3 us -> 0 us
  waiting for transfers between devices: 33.1 us -> 0 us
  starting transfers between devices: 10.2 us -> 0 us
  other arithmetic: 6.6 us -> 0 us
    pallas_call x0 -> x1, Pallas kernels: none -> 46.8 us  [shards(): pl.pallas_call(kernel, out_shape=jax.ShapeDtypeStruct((rows, width), bf16...]
    psum x1 -> x0, blocking collectives: 33.3 us -> none  [shards(): mixed = lax.psum(partial_terms, 'head').astype(jnp.bfloat16)]
    ppermute x4 -> x0, waiting for transfers between devices: 33.1 us -> none  [from_behind(): return lax.ppermute(value, axis, pairs)]
    dot_general x2 -> x0, matrix products: 28.5 us -> none  [the longest x1 15.7 us: one_block(): jnp.einsum('kgqp,pkd->qkgd', weights, value_mat, preferred_element_type=j...]
    sub x1 -> x0, matrix products: 13.4 us -> none  [one_block(): expo = jnp.where(allowed, jnp.exp(masked - row_max), 0.0)]
    ppermute x4 -> x0, starting transfers between devices: 10.2 us -> none  [from_behind(): return lax.ppermute(value, axis, pairs)]
    concatenate x2 -> x0, other arithmetic: 3.92 us -> none  [the longest x1 2.46 us: shards(): keys_ext = jnp.concatenate([piece[0] for piece in pieces] + [keys], axis=0)]
    unnamed x7 -> x1, local copies, waits for them, and re-layouts: 2.05 us -> 5.36 us
  transfers between devices with their start and end apart: 4 -> 0, of which waited for: 2 -> 0; matrix products, arithmetic and copies ran while one was open for 6% -> 0% of each run, Pallas kernels for 0% -> 0%
where the time goes in v1:
time: 52.4 us; the launch traced here: 52.1 us
  Pallas kernels  46.8 us (89%)
  local copies, waits for them, and re-layouts  5.36 us (10%)
    pallas_call x1, Pallas kernels, shards(): pl.pallas_call(kernel, out_shape=jax.ShapeDtypeStruct((rows, width), bf16...  46.8 us
    unnamed x1, local copies, waits for them, and re-layouts  5.36 us

profile of v1, /device:TPU:17, one launch (start us, length us, event | category | flops | bytes accessed | tf_op | source)
XLA Modules:
  0.0 52.1 jit_solution(15044109318488955850)
XLA Ops:
  0.0 46.8 %shard_map.55 = bf16[512,5376]{1,0:T(8,128)(2,1)} custom-call(bf16[512,1024]{1,0:T(8,128)(2,1)} %q_hbm.1, bf16[512,512]{1,0:T(8,128)(2,1)} %k_hbm.1, bf16[512,512]{1,0:T(8,128)(2,1)} %v_hbm.1, s32[8,1,512]{2,1,0:T(1,128)} %bitcast.1, bf16[1024,5376]{1,0:T(8,128)(2,1)} %w_hbm.1), custom_call_target="tpu_custom_call" | custom-call | tf_op jit(solution)/shard_map/pallas_call | solution.py:269
  46.8 5.4 %copy.7 = bf16[512,5376]{1,0:T(8,128)(2,1)} copy(bf16[512,5376]{1,0:T(8,128)(2,1)} %shard_map.55) | data formatting | bytes 11010048

commit v2 on v1

--- a/solution.py
+++ b/solution.py
@@ -21,10 +21,10 @@
 
 
 def kernel(
-    q_hbm, k_hbm, v_hbm, seg_ref, w_hbm, out_hbm,
-    q_s, k_s, v_s, w_own, w_peer, att_own, att_peer, acc, stage, bias,
+    q_hbm, k_hbm, v_hbm, seg_ref, w_hbm, out_ref,
+    q_s, k_s, v_s, w_own, w_peer, att_own, att_peer, acc, part, part_top, bias,
     q_sem, kv_sem, w_sem, ws_sem, wr_sem, zs_sem, zr_sem, ys_sem, yr_sem,
-    as_sem, ar_sem, ol_sem, os_sem, or_sem,
+    as_sem, ar_sem, os_sem, or_sem,
 ):
     heads = k_s.shape[0]
     group = q_s.shape[0] // heads
@@ -88,18 +88,13 @@
             send_sem=as_sem.at[h], recv_sem=ar_sem.at[h],
             device_id={"head": other}, device_id_type=MESH)
 
-    def out_view(at, width, owner):
-        return out_hbm.at[:, pl.ds(pl.multiple_of(owner * half + at, HEAD_SIZE), width)]
-
-    def out_local(n):
+    def out_view(n):
         at, width = chunks[n]
-        return pltpu.make_async_copy(
-            stage.at[:, pl.ds(at, width)], out_view(at, width, core), ol_sem.at[n])
+        return out_ref.at[:, pl.ds(pl.multiple_of(core * half + at, HEAD_SIZE), width)]
 
     def out_send(n):
-        at, width = chunks[n]
-        return pltpu.make_async_remote_copy(
-            src_ref=stage.at[:, pl.ds(at, width)], dst_ref=out_view(at, width, core),
+        return pltpu.make_async_remote_copy(
+            src_ref=out_view(n), dst_ref=out_view(n),
             send_sem=os_sem.at[n], recv_sem=or_sem.at[n],
             device_id={"head": other}, device_id_type=MESH)
 
@@ -160,68 +155,100 @@
         [seg_ref[jnp.maximum(seq - 2, 0)], seg_ref[jnp.maximum(seq - 1, 0)], seg_own], axis=1)
     for b in range(rows // tile):
         seg_key = seg_all[:, b * tile:b * tile + span]
-        for part in range(tile // 128):
-            lo = b * tile + part * 128
+        for piece in range(tile // 128):
+            lo = b * tile + piece * 128
             seg_query = jnp.broadcast_to(
                 seg_own[:, lo:lo + 128].astype(jnp.float32), (128, 128)).T[:, :1]
-            r = part * 128 + lax.broadcasted_iota(jnp.int32, (128, span), 0)
+            r = piece * 128 + lax.broadcasted_iota(jnp.int32, (128, span), 0)
             c = lax.broadcasted_iota(jnp.int32, (128, span), 1)
             position = seq * rows - ATTENTION_SPAN + b * tile + c
             allowed = (
                 (c <= r + ATTENTION_SPAN) & (c > r) & (position >= 0)
                 & (seg_key.astype(jnp.float32) == seg_query)
             )
-            bias[b, part * 128:(part + 1) * 128, :] = jnp.where(allowed, 0.0, -1e30)
+            bias[b, piece * 128:(piece + 1) * 128, :] = jnp.where(allowed, 0.0, -1e30)
 
     factor = SCALAR ** (-0.5) * LOG2E
-    ones = jnp.ones((span, HEAD_SIZE), jnp.bfloat16)
-
-    def product(first, last, at, width):
-        own = jnp.concatenate([att_own[n] for n in range(first, last)], axis=1)
-        far_side = jnp.concatenate([att_peer[n] for n in range(first, last)], axis=1)
-        top = slice(first * group * HEAD_SIZE, last * group * HEAD_SIZE)
-        cols = slice(at, at + width)
-        return jnp.dot(own, w_own[top, cols], preferred_element_type=jnp.float32) + jnp.dot(
-            far_side, w_peer[top, cols], preferred_element_type=jnp.float32)
+    halo = 2 * rows
+
+    def with_ones(value):
+        return jnp.concatenate([value, jnp.ones(value.shape, value.dtype)], axis=1)
+
+    def score(query, key, added):
+        return lax.dot_general(
+            query, key, (((1,), (1,)), ((), ())), preferred_element_type=jnp.float32) + added
+
+    def product(h, at, width):
+        top = pl.ds(pl.multiple_of(h * (group * HEAD_SIZE), group * HEAD_SIZE), group * HEAD_SIZE)
+        left = jnp.concatenate([att_own[h], att_peer[h]], axis=1)
+        right = jnp.concatenate(
+            [w_own[top, at:at + width], w_peer[top, at:at + width]], axis=0)
+        return jnp.dot(left, right, preferred_element_type=jnp.float32)
+
+    def inner_step(h, carry):
+        for which in range(2):
+            local_kv(which, h).wait()
+        for g in range(group):
+            local_q(h * group + g).wait()
+        for b in range(rows // tile):
+            inside = (b + 1) * tile
+            key = k_s[h, halo:halo + inside, :]
+            value = with_ones(v_s[h, halo:halo + inside, :])
+            for g in range(group):
+                n = h * group + g
+                scores = score(
+                    q_s[n, b * tile:(b + 1) * tile, :], key, bias[b, :, halo - b * tile:])
+                top = jnp.max(scores, axis=1, keepdims=True)
+                weights = jnp.exp2((scores - top) * factor).astype(jnp.bfloat16)
+                part[n, b * tile:(b + 1) * tile, :] = jnp.dot(
+                    weights, value, preferred_element_type=jnp.float32)
+                part_top[n, b * tile:(b + 1) * tile, :] = jnp.broadcast_to(
+                    top, (tile, HEAD_SIZE))
+        return carry
+
+    lax.fori_loop(0, heads, inner_step, 0)
+    acc[...] = jnp.zeros_like(acc)
 
     def step(h, carry):
-        @pl.when(h == heads - 1)
+        for which in range(2):
+            @pl.when(has_down)
+            def _():
+                far(which, h).wait_recv()
+
+            @pl.when(relays)
+            def _():
+                relay(which, h).start()
+
+        @pl.when(h == 1)
         def _():
             weight_local().wait()
             weight_send().wait_recv()
-            for n in range(heads - 1):
-                attended_send(n).wait_recv()
+
+        @pl.when(h >= 1)
+        def _():
+            attended_send(h - 1).wait_recv()
             for at, width in chunks:
-                acc[:, at:at + width] = product(0, heads - 1, at, width)
-
-        for which in range(2):
-            @pl.when(has_down)
-            def _():
-                far(which, h).wait_recv()
-
-            @pl.when(relays)
-            def _():
-                relay(which, h).start()
-
-        for which in range(2):
-            local_kv(which, h).wait()
-
+                acc[:, at:at + width] += product(h - 1, at, width)
+
+        for which in range(2):
             @pl.when(gets_near)
             def _():
                 near(which, h).wait_recv()
-        for g in range(group):
-            local_q(h * group + g).wait()
+
         for b in range(rows // tile):
-            key = k_s[h, b * tile:b * tile + span, :]
-            value = jnp.concatenate([v_s[h, b * tile:b * tile + span, :], ones], axis=1)
+            key = k_s[h, b * tile:halo, :]
+            value = with_ones(v_s[h, b * tile:halo, :])
             for g in range(group):
-                query = q_s[h * group + g, b * tile:(b + 1) * tile, :]
-                scores = lax.dot_general(
-                    query, key, (((1,), (1,)), ((), ())), preferred_element_type=jnp.float32)
-                scores = scores + bias[b]
-                top = jnp.max(scores, axis=1, keepdims=True)
+                n = h * group + g
+                scores = score(
+                    q_s[n, b * tile:(b + 1) * tile, :], key, bias[b, :, :halo - b * tile])
+                before = part_top[n, b * tile:(b + 1) * tile, :]
+                top = jnp.maximum(jnp.max(scores, axis=1, keepdims=True), before[:, :1])
                 weights = jnp.exp2((scores - top) * factor).astype(jnp.bfloat16)
-                mix = jnp.dot(weights, value, preferred_element_type=jnp.float32)
+                faded = jnp.exp2((before - top) * factor)
+                mix = part[n, b * tile:(b + 1) * tile, :] * jnp.concatenate(
+                    [faded, faded], axis=1) + jnp.dot(
+                        weights, value, preferred_element_type=jnp.float32)
                 att_own[h, b * tile:(b + 1) * tile, g * HEAD_SIZE:(g + 1) * HEAD_SIZE] = (
                     mix[:, :HEAD_SIZE] / mix[:, HEAD_SIZE:]).astype(jnp.bfloat16)
         attended_send(h).start()
@@ -231,9 +258,8 @@
 
     attended_send(heads - 1).wait_recv()
     for n, (at, width) in enumerate(chunks):
-        stage[:, at:at + width] = (
-            acc[:, at:at + width] + product(heads - 1, heads, at, width)).astype(jnp.bfloat16)
-        out_local(n).start()
+        out_view(n)[...] = (
+            acc[:, at:at + width] + product(heads - 1, at, width)).astype(jnp.bfloat16)
         out_send(n).start()
 
     for h in range(heads):
@@ -248,7 +274,6 @@
                 near(which, h).wait_send()
     weight_send().wait_send()
     for n in range(len(chunks)):
-        out_local(n).wait()
         out_send(n).wait()
 
 
@@ -263,14 +288,14 @@
     pieces = len(column_chunks(half))
     seg = segments.reshape(segments.shape[0] // rows, 1, rows)
     dma = pltpu.SemaphoreType.DMA
-    anywhere = pl.BlockSpec(memory_space=pl.ANY)
+    anywhere = pl.BlockSpec(memory_space=pltpu.HBM)
     bf16 = jnp.bfloat16
     span = ATTENTION_SPAN + QUERY_TILE
     return pl.pallas_call(
         kernel,
-        out_shape=jax.ShapeDtypeStruct((rows, width), bf16),
+        out_shape=pltpu.VMEM((rows, width), bf16),
         in_specs=[anywhere, anywhere, anywhere, pl.BlockSpec(memory_space=pltpu.VMEM), anywhere],
-        out_specs=anywhere,
+        out_specs=pl.BlockSpec(memory_space=pltpu.VMEM),
         scratch_shapes=[
             pltpu.VMEM((query_heads, rows, HEAD_SIZE), bf16),
             pltpu.VMEM((heads, 3 * rows, HEAD_SIZE), bf16),
@@ -280,14 +305,15 @@
             pltpu.VMEM((heads, rows, group * HEAD_SIZE), bf16),
             pltpu.VMEM((heads, rows, group * HEAD_SIZE), bf16),
             pltpu.VMEM((rows, half), jnp.float32),
-            pltpu.VMEM((rows, half), bf16),
+            pltpu.VMEM((query_heads, rows, 2 * HEAD_SIZE), jnp.float32),
+            pltpu.VMEM((query_heads, rows, HEAD_SIZE), jnp.float32),
             pltpu.VMEM((rows // QUERY_TILE, QUERY_TILE, span), jnp.float32),
             dma((query_heads,)), dma((2, heads)), dma, dma, dma,
             dma((2, heads)), dma((2, heads)), dma((2, heads)), dma((2, heads)),
-            dma((heads,)), dma((heads,)), dma((pieces,)), dma((pieces,)), dma((pieces,)),
+            dma((heads,)), dma((heads,)), dma((pieces,)), dma((pieces,)),
         ],
         compiler_params=pltpu.CompilerParams(
-            collective_id=0, has_side_effects=True, vmem_limit_bytes=56 * 1024 * 1024),
+            collective_id=0, has_side_effects=True, vmem_limit_bytes=55 * 1024 * 1024),
     )(queries, keys, values, seg, out_weight)
 
 

time: 52.4 us -> 45 us (0.86)
  Pallas kernels: 46.8 us -> 42.3 us
  local copies, waits for them, and re-layouts: 5.36 us -> 2.45 us
    pallas_call x1, Pallas kernels: 46.8 us -> 42.3 us  [shards(): pl.pallas_call(kernel, out_shape=pltpu.VMEM((rows, width), bf16), in_spec...]
    unnamed x1, local copies, waits for them, and re-layouts: 5.36 us -> 2.45 us
where the time goes in v2:
time: 45 us; the launch traced here: 44.7 us
  Pallas kernels  42.3 us (94%)
  local copies, waits for them, and re-layouts  2.45 us (5%)
    pallas_call x1, Pallas kernels, shards(): pl.pallas_call(kernel, out_shape=pltpu.VMEM((rows, width), bf16), in_spec...  42.3 us
    unnamed x1, local copies, waits for them, and re-layouts  2.45 us

profile of v2, /device:TPU:17, one launch (start us, length us, event | category | flops | bytes accessed | tf_op | source)
XLA Modules:
  0.0 44.7 jit_solution(748138678229809590)
XLA Ops:
  0.0 42.3 %shard_map.55 = bf16[512,5376]{1,0:T(8,128)(2,1)S(1)} custom-call(bf16[512,1024]{1,0:T(8,128)(2,1)} %q_hbm.1, bf16[512,512]{1,0:T(8,128)(2,1)} %k_hbm.1, bf16[512,512]{1,0:T(8,128)(2,1)} %v_hbm.1, s32[8,1,512]{2,1,0:T(1,128)} %bitcast.1, bf16[1024,5376]{1,0:T(8,128)(2,1)} %w_hbm.1), custom_call_target="tpu_custom_call" | custom-call | tf_op jit(solution)/shard_map/pallas_call | solution.py:294
  42.3 2.4 %copy.7 = bf16[512,5376]{1,0:T(8,128)(2,1)} copy(bf16[512,5376]{1,0:T(8,128)(2,1)S(1)} %shard_map.55) | data formatting | bytes 11010048

commit v3 on v2

--- a/solution.py
+++ b/solution.py
@@ -48,27 +48,29 @@
         return pltpu.make_async_copy(
             q_hbm.at[:, pl.ds(n * HEAD_SIZE, HEAD_SIZE)], q_s.at[n], q_sem.at[n])
 
+    piece = rows // 2
+
     def far(which, h):
-        src, dst = ((k_hbm, k_s), (v_hbm, v_s))[which]
-        return pltpu.make_async_remote_copy(
-            src_ref=src.at[:, pl.ds(h * HEAD_SIZE, HEAD_SIZE)],
-            dst_ref=dst.at[h, pl.ds(0, rows), :],
+        src, dst = ((k_hbm, k_s), (v_hbm, v_s))[which // 2]
+        return pltpu.make_async_remote_copy(
+            src_ref=src.at[pl.ds(which % 2 * piece, piece), pl.ds(h * HEAD_SIZE, HEAD_SIZE)],
+            dst_ref=dst.at[h, pl.ds(which % 2 * piece, piece), :],
             send_sem=zs_sem.at[which, h], recv_sem=zr_sem.at[which, h],
             device_id={"seq": seq + 2}, device_id_type=MESH)
 
     def near(which, h):
-        src, dst = ((k_hbm, k_s), (v_hbm, v_s))[which]
-        return pltpu.make_async_remote_copy(
-            src_ref=src.at[:, pl.ds(h * HEAD_SIZE, HEAD_SIZE)],
-            dst_ref=dst.at[h, pl.ds(rows, rows), :],
+        src, dst = ((k_hbm, k_s), (v_hbm, v_s))[which // 2]
+        return pltpu.make_async_remote_copy(
+            src_ref=src.at[pl.ds(which % 2 * piece, piece), pl.ds(h * HEAD_SIZE, HEAD_SIZE)],
+            dst_ref=dst.at[h, pl.ds(rows + which % 2 * piece, piece), :],
             send_sem=ys_sem.at[which, h], recv_sem=yr_sem.at[which, h],
             device_id={"seq": pair}, device_id_type=MESH)
 
     def relay(which, h):
-        dst = (k_s, v_s)[which]
-        return pltpu.make_async_remote_copy(
-            src_ref=dst.at[h, pl.ds(0, rows), :],
-            dst_ref=dst.at[h, pl.ds(rows, rows), :],
+        dst = (k_s, v_s)[which // 2]
+        return pltpu.make_async_remote_copy(
+            src_ref=dst.at[h, pl.ds(which % 2 * piece, piece), :],
+            dst_ref=dst.at[h, pl.ds(rows + which % 2 * piece, piece), :],
             send_sem=ys_sem.at[which, h], recv_sem=yr_sem.at[which, h],
             device_id={"seq": pair}, device_id_type=MESH)
 
@@ -121,7 +123,7 @@
         barrier, 2 + jnp.minimum(peers - 1 - seq, 2) // 2 + jnp.minimum(seq, 2) // 2)
 
     for h in range(heads):
-        for which in range(2):
+        for which in range(4):
             @pl.when(has_up)
             def _():
                 far(which, h).start()
@@ -155,18 +157,18 @@
         [seg_ref[jnp.maximum(seq - 2, 0)], seg_ref[jnp.maximum(seq - 1, 0)], seg_own], axis=1)
     for b in range(rows // tile):
         seg_key = seg_all[:, b * tile:b * tile + span]
-        for piece in range(tile // 128):
-            lo = b * tile + piece * 128
+        for strip in range(tile // 128):
+            lo = b * tile + strip * 128
             seg_query = jnp.broadcast_to(
                 seg_own[:, lo:lo + 128].astype(jnp.float32), (128, 128)).T[:, :1]
-            r = piece * 128 + lax.broadcasted_iota(jnp.int32, (128, span), 0)
+            r = strip * 128 + lax.broadcasted_iota(jnp.int32, (128, span), 0)
             c = lax.broadcasted_iota(jnp.int32, (128, span), 1)
             position = seq * rows - ATTENTION_SPAN + b * tile + c
             allowed = (
                 (c <= r + ATTENTION_SPAN) & (c > r) & (position >= 0)
                 & (seg_key.astype(jnp.float32) == seg_query)
             )
-            bias[b, piece * 128:(piece + 1) * 128, :] = jnp.where(allowed, 0.0, -1e30)
+            bias[b, strip * 128:(strip + 1) * 128, :] = jnp.where(allowed, 0.0, -1e30)
 
     factor = SCALAR ** (-0.5) * LOG2E
     halo = 2 * rows
@@ -210,7 +212,7 @@
     acc[...] = jnp.zeros_like(acc)
 
     def step(h, carry):
-        for which in range(2):
+        for which in range(4):
             @pl.when(has_down)
             def _():
                 far(which, h).wait_recv()
@@ -230,7 +232,7 @@
             for at, width in chunks:
                 acc[:, at:at + width] += product(h - 1, at, width)
 
-        for which in range(2):
+        for which in range(4):
             @pl.when(gets_near)
             def _():
                 near(which, h).wait_recv()
@@ -264,7 +266,7 @@
 
     for h in range(heads):
         attended_send(h).wait_send()
-        for which in range(2):
+        for which in range(4):
             @pl.when(has_up)
             def _():
                 far(which, h).wait_send()
@@ -309,7 +311,7 @@
             pltpu.VMEM((query_heads, rows, HEAD_SIZE), jnp.float32),
             pltpu.VMEM((rows // QUERY_TILE, QUERY_TILE, span), jnp.float32),
             dma((query_heads,)), dma((2, heads)), dma, dma, dma,
-            dma((2, heads)), dma((2, heads)), dma((2, heads)), dma((2, heads)),
+            dma((4, heads)), dma((4, heads)), dma((4, heads)), dma((4, heads)),
             dma((heads,)), dma((heads,)), dma((pieces,)), dma((pieces,)),
         ],
         compiler_params=pltpu.CompilerParams(

time: 45 us -> 45.3 us (level)
  no operation moved by 1% of the time
where the time goes in v3:
time: 45.3 us; the launch traced here: 45 us
  Pallas kernels  42.6 us (94%)
  local copies, waits for them, and re-layouts  2.45 us (5%)
    pallas_call x1, Pallas kernels, shards(): pl.pallas_call(kernel, out_shape=pltpu.VMEM((rows, width), bf16), in_spec...  42.6 us
    unnamed x1, local copies, waits for them, and re-layouts  2.45 us

profile of v3, /device:TPU:17, one launch (start us, length us, event | category | flops | bytes accessed | tf_op | source)
XLA Modules:
  0.0 45.0 jit_solution(15092745097223332415)
XLA Ops:
  0.0 42.6 %shard_map.55 = bf16[512,5376]{1,0:T(8,128)(2,1)S(1)} custom-call(bf16[512,1024]{1,0:T(8,128)(2,1)} %q_hbm.1, bf16[512,512]{1,0:T(8,128)(2,1)} %k_hbm.1, bf16[512,512]{1,0:T(8,128)(2,1)} %v_hbm.1, s32[8,1,512]{2,1,0:T(1,128)} %bitcast.1, bf16[1024,5376]{1,0:T(8,128)(2,1)} %w_hbm.1), custom_call_target="tpu_custom_call" | custom-call | tf_op jit(solution)/shard_map/pallas_call | solution.py:296
  42.6 2.4 %copy.7 = bf16[512,5376]{1,0:T(8,128)(2,1)} copy(bf16[512,5376]{1,0:T(8,128)(2,1)S(1)} %shard_map.55) | data formatting | bytes 11010048
